TPU v7x, 32 devices: a whole 2x2x4 slice. The times are simulated.
32 devices in a mesh: shot: 16 (over z, y, core), rcv: 2 (over x).
Axes of the slice: x: 2, y: 2, z: 4, core: 2. Of those that a mesh axis runs over, the one named last changes fastest.
Arguments:
- record: bfloat16 [768, 131072], P('rcv', 'shot'), may hold values from -6 to 6
- shot_fire_samples: int32 [512], P('shot'), may hold values from 0 to 131071, as said below
Outputs:
- psf_gram: float32 [2, 4, 768, 768], P(None, None, 'rcv', 'shot')
Inputs may be any that keep to these rules, and one draw needn't show every extreme that they name: `shot_fire_samples`: shot s fires at a sample from s * 256 to s * 256 + 255.
All inputs are finite; a program needn't handle non-finite values.
Results may differ from a plain program's by a relative error of at most 0.0025.
Values may be sent and summed in bfloat16 or wider, within the bound.
A program may use at most 64 MiB of HBM per device.

v0:
```python
import math
import jax
import jax.numpy as jnp
from jax import lax
from jax.sharding import PartitionSpec as P

WIN = 2048
SPACING = 256
freq_bins = (24, 40, 56, 80)


def shifted(block, axis, distance):
    devices = range(lax.axis_size(axis))
    route = [(i - distance, i) for i in devices if i - distance in devices]
    return lax.ppermute(block, axis, route)


def dft_table(window_len):
    lag_index = jnp.arange(window_len, dtype=jnp.int32)
    bin_list = jnp.array(freq_bins, dtype=jnp.int32)
    turn_count = lag_index[:, None] * bin_list[None, :] % window_len
    phase_angle = 2.0 * math.pi / window_len * turn_count.astype(jnp.float32)
    dft_rows = jnp.concatenate([jnp.cos(phase_angle), -jnp.sin(phase_angle)], axis=1) / math.sqrt(
        window_len
    )
    return dft_rows.astype(jnp.bfloat16)


def shifted_tables(jitter, span):
    lag_index = jnp.arange(span, dtype=jnp.int32)[None, :] - jitter[:, None]
    inside = (lag_index >= 0) & (lag_index < WIN)
    clipped = jnp.clip(lag_index, 0, WIN - 1)
    bin_list = jnp.array(freq_bins, dtype=jnp.int32)
    turn_count = clipped[:, None, :] * bin_list[None, :, None] % WIN
    phase_angle = 2.0 * math.pi / WIN * turn_count.astype(jnp.float32)
    table = jnp.concatenate([jnp.cos(phase_angle), -jnp.sin(phase_angle)], axis=1) / math.sqrt(WIN)
    table = jnp.where(inside[:, None, :], table, 0.0)
    return table.astype(jnp.bfloat16)


def local_spectra(extended, sample_offsets, dft_rows):
    count_of_shots = sample_offsets.shape[0]
    reach_blocks = WIN // SPACING + 1
    jitter = sample_offsets - jnp.arange(count_of_shots, dtype=jnp.int32) * SPACING
    tables = shifted_tables(jitter, reach_blocks * SPACING)
    tables = tables.reshape(count_of_shots, dft_rows.shape[1], reach_blocks, SPACING)
    blocks = extended.reshape(extended.shape[0], extended.shape[1] // SPACING, SPACING)
    total = jnp.zeros((count_of_shots, dft_rows.shape[1], extended.shape[0]), jnp.float32)
    for offset in range(reach_blocks):
        record_part = blocks[:, offset : offset + count_of_shots, :]
        total = total + jnp.einsum(
            "rsu,scu->scr", record_part, tables[:, :, offset, :], preferred_element_type=jnp.float32
        )
    return total


def gram_terms(left, right):
    nfreq = len(freq_bins)
    left_re = left[:, :nfreq, :]
    left_im = left[:, nfreq:, :]
    right_re = right[:, :nfreq, :]
    right_im = right[:, nfreq:, :]
    gram_real = jnp.einsum("sfr,sfq->frq", left_re, right_re, preferred_element_type=jnp.float32)
    gram_real = gram_real + jnp.einsum(
        "sfr,sfq->frq", left_im, right_im, preferred_element_type=jnp.float32
    )
    gram_imag = jnp.einsum("sfr,sfq->frq", left_re, right_im, preferred_element_type=jnp.float32)
    gram_imag = gram_imag - jnp.einsum(
        "sfr,sfq->frq", left_im, right_re, preferred_element_type=jnp.float32
    )
    return jnp.stack([gram_real, gram_imag], axis=0)


def per_device(record, shot_fire_samples):
    trace_segment_length = record.shape[1]
    count_of_shots = shot_fire_samples.shape[0]
    dft_rows = dft_table(WIN)
    sample_offsets = shot_fire_samples - lax.axis_index("shot") * trace_segment_length
    head_rows = record[:, :WIN]
    rim_rows = shifted(head_rows, "shot", -1)
    extended = jnp.concatenate([record, rim_rows], axis=1)
    trace_spectra = local_spectra(extended, sample_offsets, dft_rows)
    trace_spectra = trace_spectra.astype(jnp.bfloat16)
    all_receivers = lax.all_gather(trace_spectra, "rcv", axis=2, tiled=True)
    total_shots = count_of_shots * lax.axis_size("shot")
    row_side = lax.all_gather(trace_spectra, "shot", axis=0, tiled=True)
    column_side = lax.all_to_all(all_receivers, "shot", split_axis=2, concat_axis=0, tiled=True)
    result = gram_terms(row_side, column_side)
    return result / total_shots


def solution(mesh):
    return jax.shard_map(
        per_device,
        mesh=mesh,
        in_specs=(P("rcv", "shot"), P("shot")),
        out_specs=P(None, None, "rcv", "shot"),
        check_vma=False,
    )
```

profile of v0, /device:TPU:0, one launch (start us, length us, event | category | flops | bytes accessed | tf_op | source)
XLA Modules:
  0.0 125.5 jit_solution(16879435166929564003)
XLA Ops:
  6.5 8.6 %copy.41 = bf16[384,8192]{0,1:T(8,128)(2,1)} copy(bf16[384,8192]{1,0:T(8,128)(2,1)} %param.3) | data formatting | bytes 12582912 | tf_op args[0]
  15.2 1.6 %slice.93 = bf16[384,2048]{0,1:T(8,128)(2,1)S(1)} slice(bf16[384,8192]{0,1:T(8,128)(2,1)} %copy.41), slice={[0:384], [0:2048]} | slice | bytes 3145728 | tf_op jit(solution)/shard_map/slice | solution.py:79
  16.8 1.3 %collective-permute-start = (bf16[384,2048]{0,1:T(8,128)(2,1)S(1)}, bf16[384,2048]{0,1:T(8,128)(2,1)S(1)}, u32[]{:S(2)}, u32[]{:S(2)}) collective-permute-start(bf16[384,2048]{0,1:T(8,128)(2,1)S(1)} %slice.93), channel_id=1, source_target_pairs={{2,0},{4,2},{6,4},{8,6},{10,8},{12,10},{14,12},{16,14},{18,16},{20... | collective-permute-start | bytes 4718600 | tf_op jit(solution)/shard_map/ppermute | solution.py:15
  18.1 0.1 fusion.71
  18.3 0.1 subtract_clamp_fusion
  18.4 9.7 %fusion.70 = (f32[32,4,9,256]{3,1,0,2:T(4,128)S(1)}, f32[32,4,9,256]{3,1,0,2:T(4,128)S(1)}) fusion(s32[4]{0:T(128)S(1)} %copy-done.1, s32[32,9,256]{2,0,1:T(8,128)S(1)} %subtract_clamp_fusion), kind=kLoop, calls=%fused_computation.54 | loop fusion | flops 4423680 | bytes 2654224 | tf_op jit(solution)/shard_map/cos | solution.py:36
  28.1 0.8 fusion.19
  29.0 14.8 %pad_maximum_fusion = bf16[384,10240]{0,1:T(8,128)(2,1)S(1)} fusion(bf16[384,2048]{0,1:T(8,128)(2,1)S(1)} %collective-permute-done, bf16[384,8192]{0,1:T(8,128)(2,1)S(1)} %copy-done), kind=kLoop, calls=%fused_computation | loop fusion | flops 15728640 | bytes 15728640 | tf_op jit(solution)/shard_map/concatenate | solution.py:81
  43.9 0.9 fusion
  44.8 0.9 fusion.2
  45.7 0.9 fusion.4
  46.6 0.9 fusion.6
  47.6 0.9 fusion.8
  48.5 0.9 fusion.10
  49.4 0.9 fusion.12
  50.4 0.9 fusion.14
  51.3 1.6 %fusion.55 = bf16[32,8,384]{2,1,0:T(8,128)(2,1)} fusion(f32[32,8,384]{2,1,0:T(8,128)S(1)} %fusion, f32[32,8,384]{2,1,0:T(8,128)S(1)} %fusion.2, f32[32,8,384]{2,1,0:T(8,128)S(1)} %fusion.4, f32[32,8,384]{2,1,0:T(8,128)S(1)} %fusion.6, f32[32,8,384]{2,1,0:T(8,128)S(1)} %fusion.8, f32[32,8,384]{2,1,0:T(8,128)S(1)} %fusion.10, f32[32,8,384]{2,1,0:T(8,128)S(1)} %fusion.12, ...), kind=kOutput, calls=%fused_computation.48 | convolution fusion | flops 51216384 | bytes 9764864 | tf_op jit(solution)/shard_map/rsu,scu->scr/dot_general | solution.py:51
  52.9 0.0 all-gather.2.cloned.1.call-update
  52.9 7.5 %all_gather.7 = bf16[32,8,768]{2,1,0:T(8,128)(2,1)S(1)} all-gather(bf16[32,8,384]{2,1,0:T(8,128)(2,1)} %fusion.55), channel_id=1, replica_groups=mesh['shot'=16,'rcv'=2] {'rcv'}, dimensions={2}, use_global_device_ids=true | all-gather | bytes 589824 | tf_op jit(solution)/shard_map/all_gather | solution.py:84
  60.5 1.2 copy.52
  61.6 1.5 %reshape.59 = bf16[16,2,6144]{2,1,0:T(2,128)(2,1)S(1)} reshape(bf16[768,8,32]{2,1,0:T(8,128)(2,1)S(1)} %bitcast.53) | data formatting | bytes 786432
  63.1 28.9 %all_to_all.18 = bf16[16,2,6144]{2,1,0:T(2,128)(2,1)S(1)} all-to-all(bf16[16,2,6144]{2,1,0:T(2,128)(2,1)S(1)} %reshape.59), channel_id=1, replica_groups=mesh['shot'=16,'rcv'=2] {'shot'}, dimensions={0} | all-to-all | bytes 786432 | tf_op jit(solution)/shard_map/all_to_all | solution.py:87
  92.1 0.8 reshape.60
  92.8 1.0 copy.83
  93.8 1.5 %all_to_all.16 = bf16[512,8,48]{0,2,1:T(8,128)(2,1)S(1)} reshape(bf16[16,32,8,48]{1,0,3,2:T(8,128)(2,1)S(1)} %bitcast.52) | data formatting | bytes 786432 | tf_op jit(solution)/shard_map/all_to_all | solution.py:87
  95.3 16.9 %all-gather.2.cloned.1.call-done = bf16[512,8,384]{2,1,0:T(8,128)(2,1)} async-done(((bf16[32,8,384]{2,1,0:T(8,128)(2,1)}), bf16[512,8,384]{2,1,0:T(8,128)(2,1)}) %all-gather.2.cloned.1.call-update) | async-done | bytes 3145744 | tf_op jit(solution)/shard_map/all_gather | solution.py:86
  112.3 4.1 %fusion.76 = (bf16[512,4,384]{2,1,0:T(4,128)(2,1)S(1)}, bf16[512,4,384]{2,1,0:T(4,128)(2,1)S(1)}) fusion(bf16[512,8,384]{2,1,0:T(8,128)(2,1)} %all-gather.2.cloned.1.call-done), kind=kLoop, calls=%fused_computation.74 | loop fusion | bytes 6291456 | tf_op jit(solution)/shard_map/slice | solution.py:59
  116.3 0.4 fusion.22
  116.7 0.4 fusion.20
  117.1 0.4 fusion.67
  117.4 0.4 fusion.64
  117.8 0.9 maximum_multiply_fusion.1
  (10 shorter events, 0.0 us)
Async XLA Ops:
  6.5 105.7 %all-gather.2.cloned.1.call-start = ((), (), s32[]{:S(2)}) async-start(), calls=%async_computation.1 | async-start | bytes 3342336 | tf_op jit(solution)/shard_map/all_gather | solution.py:86
  15.2 2.9 %copy-start.2 = (s32[32]{0:T(128)S(1)}, s32[32]{0:T(128)}, u32[]{:S(2)}) copy-start(s32[32]{0:T(128)} %param.4) | copy-start | bytes 388
  15.2 3.2 %copy-start.1 = (s32[4]{0:T(128)S(1)}, s32[4]{0:T(128)}, u32[]{:S(2)}) copy-start(s32[4]{0:T(128)} %constant.43.clone) | copy-start | bytes 52
  16.8 12.2 %collective-permute-start = (bf16[384,2048]{0,1:T(8,128)(2,1)S(1)}, bf16[384,2048]{0,1:T(8,128)(2,1)S(1)}, u32[]{:S(2)}, u32[]{:S(2)}) collective-permute-start(bf16[384,2048]{0,1:T(8,128)(2,1)S(1)} %slice.93), channel_id=1, source_target_pairs={{2,0},{4,2},{6,4},{8,6},{10,8},{12,10},{14,12},{16,14},{18,16},{20... | collective-permute-start | bytes 4718600 | tf_op jit(solution)/shard_map/ppermute | solution.py:15
  18.3 10.8 %copy-start = (bf16[384,8192]{0,1:T(8,128)(2,1)S(1)}, bf16[384,8192]{0,1:T(8,128)(2,1)}, u32[]{:S(2)}) copy-start(bf16[384,8192]{0,1:T(8,128)(2,1)} %copy.41) | copy-start | bytes 18874372
Sparse Core Ops, SparseCore 0:
  53.0 59.1 all-gather.1
where the time goes:
time: 126 us
  blocking collectives  36.5 us (29%)
  other arithmetic  26.6 us (21%)
  local copies, waits for them, and re-layouts  20.2 us (16%)
  waiting for transfers between devices  17 us (13%)
  between operations  13.6 us (11%)
  matrix products  10.5 us (8%)
  starting transfers between devices  1.29 us (1%)
    all_to_all x1, blocking collectives, per_device(): lax.all_to_all(all_receivers, 'shot', split_axis=2, concat_axis=0, tiled=...  28.9 us
    all_gather x1, waiting for transfers between devices, per_device(): row_side = lax.all_gather(trace_spectra, 'shot', axis=0, tiled=True)  16.9 us
    concatenate x1, other arithmetic, per_device(): extended = jnp.concatenate([record, rim_rows], axis=1)  14.8 us
    unnamed x9, local copies, waits for them, and re-layouts  10.9 us
    cos x1, other arithmetic, shifted_tables(): jnp.cos(phase_angle)  9.74 us
    dot_general x9, matrix products, local_spectra(): jnp.einsum('rsu,scu->scr', record_part, tables[:, :, offset, :], preferre...  9.03 us
    all_gather x1, blocking collectives, per_device(): all_receivers = lax.all_gather(trace_spectra, 'rcv', axis=2, tiled=True)  7.55 us
    slice x1, local copies, waits for them, and re-layouts, gram_terms(): left_re = left[:, :nfreq, :]  4.06 us
  transfers between devices with their start and end apart: 2, of which 1 were waited for; matrix products, arithmetic and copies ran while one was open for 12% of the time, Pallas kernels for 0%

commit v1 on v0

--- a/solution.py
+++ b/solution.py
@@ -1,3 +1,4 @@
+import functools
 import math
 import jax
 import jax.numpy as jnp
@@ -7,6 +8,13 @@
 WIN = 2048
 SPACING = 256
 freq_bins = (24, 40, 56, 80)
+
+
+def store_core_on(vec, row_axis):
+    return jnp.concatenate(lax.all_gather(vec, axis_name=row_axis), 2)
+
+
+define_targets = functools.partial(store_core_on, row_axis="rcv")
 
 
 def shifted(block, axis, distance):
@@ -81,7 +89,7 @@
     extended = jnp.concatenate([record, rim_rows], axis=1)
     trace_spectra = local_spectra(extended, sample_offsets, dft_rows)
     trace_spectra = trace_spectra.astype(jnp.bfloat16)
-    all_receivers = lax.all_gather(trace_spectra, "rcv", axis=2, tiled=True)
+    all_receivers = define_targets(trace_spectra)
     total_shots = count_of_shots * lax.axis_size("shot")
     row_side = lax.all_gather(trace_spectra, "shot", axis=0, tiled=True)
     column_side = lax.all_to_all(all_receivers, "shot", split_axis=2, concat_axis=0, tiled=True)

time: 126 us -> 126 us (level)
    reshape x0 -> x1, local copies, waits for them, and re-layouts: none -> 1.34 us  [store_core_on(): return jnp.concatenate(lax.all_gather(vec, axis_name=row_axis), 2)]
  transfers between devices with their start and end apart: 2 -> 2, of which waited for: 1 -> 1; matrix products, arithmetic and copies ran while one was open for 12% -> 13% of each run, Pallas kernels for 0% -> 0%
where the time goes in v1:
time: 126 us
  blocking collectives  36.5 us (29%)
  other arithmetic  26.6 us (21%)
  local copies, waits for them, and re-layouts  20.8 us (17%)
  waiting for transfers between devices  16.5 us (13%)
  between operations  13.6 us (11%)
  matrix products  10.5 us (8%)
  starting transfers between devices  1.29 us (1%)
    all_to_all x1, blocking collectives, per_device(): lax.all_to_all(all_receivers, 'shot', split_axis=2, concat_axis=0, tiled=...  28.9 us
    all_gather x1, waiting for transfers between devices, per_device(): row_side = lax.all_gather(trace_spectra, 'shot', axis=0, tiled=True)  16.5 us
    concatenate x1, other arithmetic, per_device(): extended = jnp.concatenate([record, rim_rows], axis=1)  14.8 us
    unnamed x9, local copies, waits for them, and re-layouts  10.9 us
    cos x1, other arithmetic, shifted_tables(): jnp.cos(phase_angle)  9.74 us
    dot_general x9, matrix products, local_spectra(): jnp.einsum('rsu,scu->scr', record_part, tables[:, :, offset, :], preferre...  9.03 us
    all_gather x1, blocking collectives, store_core_on(): return jnp.concatenate(lax.all_gather(vec, axis_name=row_axis), 2)  7.55 us
    slice x1, local copies, waits for them, and re-layouts, gram_terms(): left_re = left[:, :nfreq, :]  4.06 us
  transfers between devices with their start and end apart: 2, of which 1 were waited for; matrix products, arithmetic and copies ran while one was open for 13% of the time, Pallas kernels for 0%

profile of v1, /device:TPU:0, one launch (start us, length us, event | category | flops | bytes accessed | tf_op | source)
XLA Modules:
  0.0 125.7 jit_solution(13506873950316850135)
XLA Ops:
  6.5 8.6 %copy.43 = bf16[384,8192]{0,1:T(8,128)(2,1)} copy(bf16[384,8192]{1,0:T(8,128)(2,1)} %param.3) | data formatting | bytes 12582912 | tf_op args[0]
  15.2 1.6 %slice.93 = bf16[384,2048]{0,1:T(8,128)(2,1)S(1)} slice(bf16[384,8192]{0,1:T(8,128)(2,1)} %copy.43), slice={[0:384], [0:2048]} | slice | bytes 3145728 | tf_op jit(solution)/shard_map/slice | solution.py:87
  16.8 1.3 %collective-permute-start = (bf16[384,2048]{0,1:T(8,128)(2,1)S(1)}, bf16[384,2048]{0,1:T(8,128)(2,1)S(1)}, u32[]{:S(2)}, u32[]{:S(2)}) collective-permute-start(bf16[384,2048]{0,1:T(8,128)(2,1)S(1)} %slice.93), channel_id=1, source_target_pairs={{2,0},{4,2},{6,4},{8,6},{10,8},{12,10},{14,12},{16,14},{18,16},{20... | collective-permute-start | bytes 4718600 | tf_op jit(solution)/shard_map/ppermute | solution.py:23
  18.1 0.1 fusion.71
  18.3 0.1 subtract_clamp_fusion
  18.4 9.7 %fusion.70 = (f32[32,4,9,256]{3,1,0,2:T(4,128)S(1)}, f32[32,4,9,256]{3,1,0,2:T(4,128)S(1)}) fusion(s32[4]{0:T(128)S(1)} %copy-done.1, s32[32,9,256]{2,0,1:T(8,128)S(1)} %subtract_clamp_fusion), kind=kLoop, calls=%fused_computation.53 | loop fusion | flops 4423680 | bytes 2654224 | tf_op jit(solution)/shard_map/cos | solution.py:44
  28.1 0.8 fusion.19
  29.0 14.8 %pad_maximum_fusion = bf16[384,10240]{0,1:T(8,128)(2,1)S(1)} fusion(bf16[384,2048]{0,1:T(8,128)(2,1)S(1)} %collective-permute-done, bf16[384,8192]{0,1:T(8,128)(2,1)S(1)} %copy-done), kind=kLoop, calls=%fused_computation | loop fusion | flops 15728640 | bytes 15728640 | tf_op jit(solution)/shard_map/concatenate | solution.py:89
  43.9 0.9 fusion
  44.8 0.9 fusion.2
  45.7 0.9 fusion.4
  46.6 0.9 fusion.6
  47.6 0.9 fusion.8
  48.5 0.9 fusion.10
  49.4 0.9 fusion.12
  50.4 0.9 fusion.14
  51.3 1.6 %fusion.55 = bf16[32,8,384]{2,1,0:T(8,128)(2,1)} fusion(f32[32,8,384]{2,1,0:T(8,128)S(1)} %fusion, f32[32,8,384]{2,1,0:T(8,128)S(1)} %fusion.2, f32[32,8,384]{2,1,0:T(8,128)S(1)} %fusion.4, f32[32,8,384]{2,1,0:T(8,128)S(1)} %fusion.6, f32[32,8,384]{2,1,0:T(8,128)S(1)} %fusion.8, f32[32,8,384]{2,1,0:T(8,128)S(1)} %fusion.10, f32[32,8,384]{2,1,0:T(8,128)S(1)} %fusion.12, ...), kind=kOutput, calls=%fused_computation.47 | convolution fusion | flops 51216384 | bytes 9764864 | tf_op jit(solution)/shard_map/rsu,scu->scr/dot_general | solution.py:59
  52.9 7.5 %all-gather = bf16[64,8,384]{2,1,0:T(8,128)(2,1)S(1)} all-gather(bf16[32,8,384]{2,1,0:T(8,128)(2,1)} %fusion.55), channel_id=2, replica_groups=mesh['shot'=16,'rcv'=2] {'rcv'}, dimensions={0}, use_global_device_ids=true | all-gather | bytes 589824 | tf_op jit(solution)/shard_map/all_gather | solution.py:14
  60.5 0.4 copy.90
  60.9 1.3 %copy.59 = bf16[32,8,2,384]{0,1,3,2:T(8,128)(2,1)S(1)} copy(bf16[32,8,2,384]{3,2,1,0:T(2,128)(2,1)S(1)} %bitcast.59) | data formatting | bytes 786432 | tf_op jit(solution)/shard_map/reshape | solution.py:14
  62.2 1.5 %reshape.68 = bf16[16,2,6144]{2,1,0:T(2,128)(2,1)S(1)} reshape(bf16[768,8,32]{2,1,0:T(8,128)(2,1)S(1)} %bitcast.57) | data formatting | bytes 786432
  63.7 28.9 %all_to_all.18 = bf16[16,2,6144]{2,1,0:T(2,128)(2,1)S(1)} all-to-all(bf16[16,2,6144]{2,1,0:T(2,128)(2,1)S(1)} %reshape.68), channel_id=1, replica_groups=mesh['shot'=16,'rcv'=2] {'shot'}, dimensions={0} | all-to-all | bytes 786432 | tf_op jit(solution)/shard_map/all_to_all | solution.py:95
  92.7 0.8 reshape.69
  93.4 1.0 copy.57
  94.4 1.5 %all_to_all.16 = bf16[512,8,48]{0,2,1:T(8,128)(2,1)S(1)} reshape(bf16[16,32,8,48]{1,0,3,2:T(8,128)(2,1)S(1)} %copy.57) | data formatting | bytes 786432 | tf_op jit(solution)/shard_map/all_to_all | solution.py:95
  95.9 16.5 %all-gather.3.cloned.1.call-done = bf16[512,8,384]{2,1,0:T(8,128)(2,1)} async-done(((bf16[32,8,384]{2,1,0:T(8,128)(2,1)}), bf16[512,8,384]{2,1,0:T(8,128)(2,1)}) %all-gather.3.cloned.1.call-update) | async-done | bytes 3145744 | tf_op jit(solution)/shard_map/all_gather | solution.py:94
  112.5 4.1 %fusion.76 = (bf16[512,4,384]{2,1,0:T(4,128)(2,1)S(1)}, bf16[512,4,384]{2,1,0:T(4,128)(2,1)S(1)}) fusion(bf16[512,8,384]{2,1,0:T(8,128)(2,1)} %all-gather.3.cloned.1.call-done), kind=kLoop, calls=%fused_computation.74 | loop fusion | bytes 6291456 | tf_op jit(solution)/shard_map/slice | solution.py:67
  116.5 0.4 fusion.22
  116.9 0.4 fusion.20
  117.2 0.4 fusion.67
  117.6 0.4 fusion.64
  118.0 0.9 maximum_multiply_fusion.1
  (11 shorter events, 0.0 us)
Async XLA Ops:
  6.5 105.9 %all-gather.3.cloned.1.call-start = ((), (), s32[]{:S(2)}) async-start(), calls=%async_computation.1 | async-start | bytes 3342336 | tf_op jit(solution)/shard_map/all_gather | solution.py:94
  15.2 2.9 %copy-start.2 = (s32[32]{0:T(128)S(1)}, s32[32]{0:T(128)}, u32[]{:S(2)}) copy-start(s32[32]{0:T(128)} %param.4) | copy-start | bytes 388
  15.2 3.2 %copy-start.1 = (s32[4]{0:T(128)S(1)}, s32[4]{0:T(128)}, u32[]{:S(2)}) copy-start(s32[4]{0:T(128)} %constant.43.clone) | copy-start | bytes 52
  16.8 12.2 %collective-permute-start = (bf16[384,2048]{0,1:T(8,128)(2,1)S(1)}, bf16[384,2048]{0,1:T(8,128)(2,1)S(1)}, u32[]{:S(2)}, u32[]{:S(2)}) collective-permute-start(bf16[384,2048]{0,1:T(8,128)(2,1)S(1)} %slice.93), channel_id=1, source_target_pairs={{2,0},{4,2},{6,4},{8,6},{10,8},{12,10},{14,12},{16,14},{18,16},{20... | collective-permute-start | bytes 4718600 | tf_op jit(solution)/shard_map/ppermute | solution.py:23
  18.3 10.8 %copy-start = (bf16[384,8192]{0,1:T(8,128)(2,1)S(1)}, bf16[384,8192]{0,1:T(8,128)(2,1)}, u32[]{:S(2)}) copy-start(bf16[384,8192]{0,1:T(8,128)(2,1)} %copy.43) | copy-start | bytes 18874372
Sparse Core Ops, SparseCore 0:
  53.0 59.3 all-gather.2
